TPU v7x, 32 devices: a whole 2x2x4 slice. The times are simulated.
32 devices in a mesh: dp: 4 (over z), cp: 8 (over y, x, core).
Axes of the slice: x: 2, y: 2, z: 4, core: 2. Of those that a mesh axis runs over, the one named last changes fastest.
Arguments:
- row_owner: int32 [4096, 1], P(('dp', 'cp')), may hold values from 0 to 31; in each aligned block of 128 rows (0 to 127, 128 to 255, ...) at most 10 rows name the same one
- slot_row: int32 [4096], P(('dp', 'cp')), may hold values from 0 to 2559
- hot_table: bfloat16 [16384, 512], P(('dp', 'cp')), may hold values from -6 to 6
- cold_table: bfloat16 [65536, 128], P(('dp', 'cp')), may hold values from -6 to 6
- cold_projection: bfloat16 [128, 512], replicated, may hold values from -0.5 to 0.5
- joined_weight: bfloat16 [512, 2048], replicated, may hold values from -0.25 to 0.25
- output_weight: bfloat16 [512, 512], replicated, may hold values from -0.25 to 0.25
- cotangent: bfloat16 [4096, 512], P(('dp', 'cp')), may hold values from -6 to 6
Outputs:
- layer_out: bfloat16 [4096, 512], P(('dp', 'cp'))
- hot_gradient: float32 [16384, 512], P(('dp', 'cp'))
- cold_gradient: float32 [65536, 128], P(('dp', 'cp'))
- projection_gradient: float32 [128, 512], replicated
- joined_gradient: float32 [512, 2048], replicated
- output_gradient: float32 [512, 512], replicated
Inputs may be any that keep to these rules, and one draw needn't show every extreme that they name: `row_owner`: in each aligned block of 128 rows (the rows of one device) no owner is named by more than 10 rows.
All inputs are finite; a program needn't handle non-finite values.
Results may differ from a plain program's by a relative error of at most 0.013.
Values may be sent and summed in bfloat16 or wider, within the bound.
No kernel may reach another device: no remote copies, remote signals or barrier semaphores. Data moves between devices by JAX's collectives and lax.ppermute only.
A program may use at most 128 MiB of HBM per device.

v0:
```python
import math
import jax
import jax.numpy as jnp
from jax import lax
from jax.sharding import PartitionSpec as P

HEADS = 8
EPSILON = 1e-05
block_limit = 1024


def silu_slope(values):
    sigmoid_v = jax.nn.sigmoid(values)
    return sigmoid_v * (1.0 + values * (1.0 - sigmoid_v))


def layer_normalize(values):
    average = jnp.mean(values, axis=-1, keepdims=True)
    centred = values - average
    inverse = lax.rsqrt(jnp.mean(centred * centred, axis=-1, keepdims=True) + EPSILON)
    return (centred * inverse, inverse)


def normalize_back(gradient, normed, inverse):
    first_term = jnp.mean(gradient, axis=-1, keepdims=True)
    second_term = jnp.mean(gradient * normed, axis=-1, keepdims=True)
    return (gradient - first_term - normed * second_term) * inverse


def masked_scores(query_heads, key_heads, query_index, key_index, score_scale):
    scores = (
        jnp.einsum("qhd,khd->hqk", query_heads, key_heads, preferred_element_type=jnp.float32)
        * score_scale
    )
    allowed = (key_index[None, :] <= query_index[:, None])[None]
    weights = jnp.where(allowed, jax.nn.silu(scores), 0.0).astype(jnp.bfloat16)
    return (scores, allowed, weights)


def score_deltas(
    query_heads, key_heads, value_heads, delta_heads, query_index, key_index, score_scale
):
    scores, allowed, weights = masked_scores(
        query_heads, key_heads, query_index, key_index, score_scale
    )
    delta_weights = jnp.einsum(
        "qhd,khd->hqk", delta_heads, value_heads, preferred_element_type=jnp.float32
    )
    delta_scores = jnp.where(allowed, delta_weights * silu_slope(scores) * score_scale, 0.0).astype(
        jnp.bfloat16
    )
    return (weights, delta_scores)


def local(
    row_owner,
    slot_row,
    hot_table,
    cold_table,
    cold_projection,
    joined_weight,
    output_weight,
    cotangent,
):
    tokens_here = slot_row.shape[0]
    model_width = output_weight.shape[0]
    hot_count = hot_table.shape[0]
    cold_count = cold_table.shape[0]
    cold_width = cold_table.shape[1]
    head_count = HEADS
    head_size = model_width // head_count
    score_scale = 1.0 / math.sqrt(head_size)
    devices = lax.axis_size(("dp", "cp"))
    group_index = lax.axis_index("cp")
    capacity = 2 * tokens_here // devices + 2
    owners = row_owner[:, 0]
    is_hot = slot_row < hot_count
    is_cold = jnp.logical_not(is_hot)
    onehot = (owners[:, None] == jnp.arange(devices, dtype=jnp.int32)[None, :]).astype(jnp.bfloat16)
    lower_mask = (jnp.arange(tokens_here)[:, None] > jnp.arange(tokens_here)[None, :]).astype(
        jnp.bfloat16
    )
    earlier = jnp.dot(lower_mask, onehot, preferred_element_type=jnp.float32)
    rank_in_owner = jnp.sum(earlier * onehot.astype(jnp.float32), axis=1).astype(jnp.int32)
    slot_index = owners * capacity + rank_in_owner
    requests = (
        jnp.full((devices * capacity,), -1, jnp.int32)
        .at[slot_index]
        .set(slot_row)
        .reshape(devices, capacity)
    )
    asked_rows = lax.all_to_all(requests, ("dp", "cp"), split_axis=0, concat_axis=0, tiled=True)
    valid_hot = (asked_rows >= 0) & (asked_rows < hot_count)
    valid_cold = asked_rows >= hot_count
    nothing = jnp.zeros((), jnp.bfloat16)
    hot_pick = jnp.where(
        valid_hot[..., None], hot_table[jnp.clip(asked_rows, 0, hot_count - 1)], nothing
    )
    cold_pick = jnp.where(
        valid_cold[..., None],
        cold_table[jnp.clip(asked_rows - hot_count, 0, cold_count - 1)],
        nothing,
    )
    hot_back, cold_back = (
        lax.all_to_all(hot_pick, ("dp", "cp"), split_axis=0, concat_axis=0, tiled=True),
        lax.all_to_all(cold_pick, ("dp", "cp"), split_axis=0, concat_axis=0, tiled=True),
    )
    hot_vector = hot_back.reshape(devices * capacity, model_width)[slot_index]
    cold_vector = cold_back.reshape(devices * capacity, cold_width)[slot_index]
    cold_embed = jnp.dot(cold_vector, cold_projection, preferred_element_type=jnp.float32)
    embedded = jnp.where(is_hot[:, None], hot_vector.astype(jnp.float32), cold_embed)
    normed, inverse = layer_normalize(embedded)
    normed_low = normed.astype(jnp.bfloat16)
    hidden = jnp.dot(normed_low, joined_weight, preferred_element_type=jnp.float32)
    active = jax.nn.silu(hidden).astype(jnp.bfloat16)
    gate_part = active[:, :model_width]
    attention_rows = active[:, model_width:]
    segments = [(0, tokens_here, group_index * tokens_here)]
    value_rows = attention_rows[:, :model_width]
    query_rows = attention_rows[:, model_width : 2 * model_width]
    key_rows = attention_rows[:, 2 * model_width :]
    local_index = jnp.concatenate(
        [first + jnp.arange(count, dtype=jnp.int32) for start, count, first in segments]
    )
    all_keys, all_values = (
        lax.all_gather(key_rows, "cp", axis=0, tiled=True),
        lax.all_gather(value_rows, "cp", axis=0, tiled=True),
    )
    length = all_keys.shape[0]
    key_span = min(length, block_limit)
    heads_shape = (tokens_here, head_count, head_size)
    query_heads = query_rows.reshape(heads_shape)

    def key_slices(counter):
        offset = counter * key_span
        key_block = lax.dynamic_slice_in_dim(all_keys, offset, key_span, 0).reshape(
            key_span, head_count, head_size
        )
        value_block = lax.dynamic_slice_in_dim(all_values, offset, key_span, 0).reshape(
            key_span, head_count, head_size
        )
        key_index = offset + jnp.arange(key_span, dtype=jnp.int32)
        return (offset, key_block, value_block, key_index)

    def blocks_needed(first, count):
        return (first + count + key_span - 1) // key_span

    start, count, first = segments[0]
    segment_queries = query_heads
    segment_index = first + jnp.arange(count, dtype=jnp.int32)

    def forward_step(
        counter, running, segment_queries=segment_queries, segment_index=segment_index
    ):
        offset, key_block, value_block, key_index = key_slices(counter)
        scores, allowed, weights = masked_scores(
            segment_queries, key_block, segment_index, key_index, score_scale
        )
        return running + jnp.einsum(
            "hqk,khd->qhd", weights, value_block, preferred_element_type=jnp.float32
        )

    empty_part = jnp.zeros((count, head_count, head_size), jnp.float32)
    attended_parts = lax.fori_loop(0, blocks_needed(first, count), forward_step, empty_part)
    attended = attended_parts.reshape(tokens_here, model_width)
    mixed, inverse_mix = layer_normalize(attended)
    gated = (mixed * gate_part.astype(jnp.float32)).astype(jnp.bfloat16)
    branch = jnp.dot(gated, output_weight, preferred_element_type=jnp.float32)
    layer_out = (embedded + branch).astype(jnp.bfloat16)
    delta_gated = jnp.dot(cotangent, output_weight.T, preferred_element_type=jnp.float32)
    delta_gate = delta_gated * mixed
    delta_attended = normalize_back(
        delta_gated * gate_part.astype(jnp.float32), mixed, inverse_mix
    ).astype(jnp.bfloat16)
    delta_heads = delta_attended.reshape(heads_shape)
    empty_heads = jnp.zeros(heads_shape, jnp.float32)
    start, count, first = segments[0]
    segment_queries = query_heads
    segment_deltas = delta_heads
    segment_index = first + jnp.arange(count, dtype=jnp.int32)

    def query_step(
        counter,
        running,
        segment_queries=segment_queries,
        segment_deltas=segment_deltas,
        segment_index=segment_index,
    ):
        offset, key_block, value_block, key_index = key_slices(counter)
        weights, delta_scores = score_deltas(
            segment_queries,
            key_block,
            value_block,
            segment_deltas,
            segment_index,
            key_index,
            score_scale,
        )
        return running + jnp.einsum(
            "hqk,khd->qhd", delta_scores, key_block, preferred_element_type=jnp.float32
        )

    empty_part = jnp.zeros((count, head_count, head_size), jnp.float32)
    query_parts = lax.fori_loop(0, blocks_needed(first, count), query_step, empty_part)
    key_heads = key_rows.reshape(heads_shape)
    value_heads = value_rows.reshape(heads_shape)
    key_lowest = jnp.min(local_index)
    query_piece = lax.all_gather(query_rows, "cp", axis=0, tiled=True)
    delta_piece = lax.all_gather(delta_attended, "cp", axis=0, tiled=True)
    row_count = query_piece.shape[0]
    sub_rows = math.gcd(row_count, block_limit)

    def inner_step(counter, partial_sums):
        start_row = counter * sub_rows
        query_block = lax.dynamic_slice_in_dim(query_piece, start_row, sub_rows, 0).reshape(
            sub_rows, head_count, head_size
        )
        delta_block = lax.dynamic_slice_in_dim(delta_piece, start_row, sub_rows, 0).reshape(
            sub_rows, head_count, head_size
        )
        query_index = start_row + jnp.arange(sub_rows, dtype=jnp.int32)

        def accumulate(sums_in):
            weights, delta_scores = score_deltas(
                query_block,
                key_heads,
                value_heads,
                delta_block,
                query_index,
                local_index,
                score_scale,
            )
            key_sum = sums_in[0] + jnp.einsum(
                "hqk,qhd->khd", delta_scores, query_block, preferred_element_type=jnp.float32
            )
            value_sum = sums_in[1] + jnp.einsum(
                "hqk,qhd->khd", weights, delta_block, preferred_element_type=jnp.float32
            )
            return (key_sum, value_sum)

        return lax.cond(
            jnp.max(query_index) >= key_lowest, accumulate, lambda sums_in: sums_in, partial_sums
        )

    key_sum, value_sum = lax.fori_loop(
        0, row_count // sub_rows, inner_step, (empty_heads, empty_heads)
    )
    delta_key = key_sum.reshape(tokens_here, model_width)
    delta_value = value_sum.reshape(tokens_here, model_width)
    attention_grads = jnp.concatenate(
        [delta_value, query_parts.reshape(tokens_here, model_width), delta_key], axis=1
    )
    delta_active = jnp.concatenate([delta_gate, attention_grads], axis=1)
    delta_hidden = (delta_active * silu_slope(hidden)).astype(jnp.bfloat16)
    delta_normed = jnp.dot(delta_hidden, joined_weight.T, preferred_element_type=jnp.float32)
    delta_embed = normalize_back(delta_normed, normed, inverse) + cotangent.astype(jnp.float32)
    cold_float = jnp.where(is_cold[:, None], cold_vector.astype(jnp.float32), 0.0)
    joined_local = jnp.dot(normed_low.T, delta_hidden, preferred_element_type=jnp.float32)
    output_local = jnp.dot(gated.T, cotangent, preferred_element_type=jnp.float32)
    projection_local = jnp.dot(cold_float.T, delta_embed, precision=lax.Precision.HIGHEST)
    joined_sum, output_sum, projection_sum = lax.psum(
        (joined_local, output_local, projection_local), ("dp", "cp")
    )
    norm_scale = (tokens_here * devices) ** (-0.5)
    cold_event = jnp.where(
        is_cold[:, None],
        jnp.dot(
            delta_embed, cold_projection.astype(jnp.float32).T, precision=lax.Precision.HIGHEST
        ),
        0.0,
    )
    hot_event = jnp.where(is_hot[:, None], delta_embed, 0.0)
    hot_buffer = (
        jnp.zeros((devices * capacity, model_width), jnp.float32)
        .at[slot_index]
        .set(hot_event)
        .reshape(devices, capacity, model_width)
    )
    cold_buffer = (
        jnp.zeros((devices * capacity, cold_width), jnp.float32)
        .at[slot_index]
        .set(cold_event)
        .reshape(devices, capacity, cold_width)
    )
    hot_arrived, cold_arrived = (
        lax.all_to_all(hot_buffer, ("dp", "cp"), split_axis=0, concat_axis=0, tiled=True),
        lax.all_to_all(cold_buffer, ("dp", "cp"), split_axis=0, concat_axis=0, tiled=True),
    )
    hot_target = jnp.where(valid_hot, asked_rows, hot_count).reshape(-1)
    cold_target = jnp.where(valid_cold, asked_rows - hot_count, cold_count).reshape(-1)
    hot_gradient = (
        jnp.zeros((hot_count, model_width), jnp.float32)
        .at[hot_target]
        .add(hot_arrived.reshape(-1, model_width), mode="drop")
    )
    cold_gradient = (
        jnp.zeros((cold_count, cold_width), jnp.float32)
        .at[cold_target]
        .add(cold_arrived.reshape(-1, cold_width), mode="drop")
    )
    return (
        layer_out,
        hot_gradient,
        cold_gradient,
        projection_sum * norm_scale,
        joined_sum * norm_scale,
        output_sum * norm_scale,
    )


def solution(mesh):
    placed = (
        P(("dp", "cp"), None),
        P(("dp", "cp")),
        P(("dp", "cp"), None),
        P(("dp", "cp"), None),
        P(),
        P(),
        P(),
        P(("dp", "cp"), None),
    )
    return jax.shard_map(
        local,
        mesh=mesh,
        in_specs=placed,
        out_specs=(
            P(("dp", "cp"), None),
            P(("dp", "cp"), None),
            P(("dp", "cp"), None),
            P(),
            P(),
            P(),
        ),
        check_vma=False,
    )
```

profile of v0, /device:TPU:0, one launch (start us, length us, event | category | flops | bytes accessed | tf_op | source)
XLA Modules:
  0.0 384.5 jit_solution(10527699452270542202)
XLA Ops:
  8.9 1.1 scatter_custom_fusion
  10.7 7.3 %all-to-all-start = ((s32[32,1,10]{2,1,0:T(1,128)}), s32[32,1,10]{2,1,0:T(1,128)S(1)}, u32[]{:S(2)}, u32[]{:S(2)}) async-start(s32[32,1,10]{2,1,0:T(1,128)} %bitcast.9), calls=%async_computation | async-start | bytes 32768 | tf_op jit(solution)/shard_map/all_to_all | solution.py:92
  18.0 7.1 %all-to-all-done = s32[32,1,10]{2,1,0:T(1,128)S(1)} async-done(((s32[32,1,10]{2,1,0:T(1,128)}), s32[32,1,10]{2,1,0:T(1,128)S(1)}, u32[]{:S(2)}, u32[]{:S(2)}) %all-to-all-start) | async-done | bytes 1312 | tf_op jit(solution)/shard_map/all_to_all | solution.py:92
  26.5 2.2 gather_fusion.2
  29.6 2.6 all-to-all-start.2
  32.3 2.0 gather_fusion
  35.4 5.0 %all-to-all-done.2 = bf16[32,10,128]{2,1,0:T(8,128)(2,1)S(1)} async-done(((bf16[32,10,128]{2,1,0:T(8,128)(2,1)}), bf16[32,10,128]{2,1,0:T(8,128)(2,1)S(1)}, u32[]{:S(2)}, u32[]{:S(2)}) %all-to-all-start.2) | async-done | bytes 81952 | tf_op jit(solution)/shard_map/all_to_all | solution.py:106
  40.4 2.6 all-to-all-start.1
  44.4 14.2 %all-to-all-done.1 = bf16[32,10,512]{2,1,0:T(8,128)(2,1)S(1)} async-done(((bf16[32,10,512]{2,1,0:T(8,128)(2,1)}), bf16[32,10,512]{2,1,0:T(8,128)(2,1)S(1)}, u32[]{:S(2)}, u32[]{:S(2)}) %all-to-all-start.1) | async-done | bytes 327712 | tf_op jit(solution)/shard_map/all_to_all | solution.py:105
  60.1 1.5 multiply_convert_fusion
  66.6 18.3 %all-gather.5.cloned.1.call-done = bf16[1024,512]{1,0:T(8,128)(2,1)} async-done(((bf16[128,512]{1,0:T(8,128)(2,1)}), bf16[1024,512]{1,0:T(8,128)(2,1)}) %all-gather.5.cloned.1.call-update) | async-done | bytes 1048592 | tf_op jit(solution)/shard_map/all_gather | solution.py:126
  84.9 2.3 copy.48
  87.2 23.6 %all-gather.7.cloned.1.call-done = bf16[1024,512]{1,0:T(8,128)(2,1)} async-done(((bf16[128,512]{1,0:T(8,128)(2,1)}), bf16[1024,512]{1,0:T(8,128)(2,1)}) %all-gather.7.cloned.1.call-update) | async-done | bytes 1048592 | tf_op jit(solution)/shard_map/all_gather | solution.py:127
  110.8 1.5 copy.49
  113.0 4.2 %while.28 = (s32[]{:T(128)}, f32[128,8,64]{0,2,1:T(8,128)}, s32[]{:T(128)}, bf16[1024,512]{0,1:T(8,128)(2,1)}, bf16[128,8,64]{0,2,1:T(8,128)(2,1)}, /*index=5*/b...) while((s32[]{:T(128)}, f32[128,8,64]{0,2,1:T(8,128)}, s32[]{:T(128)}, ...), condition=%wide.region_5.6_spmd.clone, body=%wide.region_4.5_spmd.clone.sunk | while | flops 275973248 | bytes 3023985 | solution.py:164
  113.2 4.0 %fusion.115 = f32[128,8,64]{0,2,1:T(8,128)} fusion(f32[128,8,64]{0,2,1:T(8,128)} %get-tuple-element.430, bf16[1024,8,64]{0,2,1:T(8,128)(2,1)S(1)} %bitcast.111, bf16[128,8,64]{0,2,1:T(8,128)(2,1)} %get-tuple-element.442, bf16[1024,8,64]{0,2,1:T(8,128)(2,1)} %bitcast.117, pred[128,1024]{1,0:T(8,128)(4,1)S(1)} %broadcast_compare_fusion.6), kind=kOutput, calls=%fused_computation.30.clone.1 | convolution fusion | flops 275841024 | bytes 2883584 | tf_op jit(solution)/shard_map/while/body/hqk,khd->qhd/dot_general | solution.py:159
  118.2 1.8 copy.50
  121.1 1.6 fusion.45
  122.7 2.0 multiply_convert_fusion.1
  126.5 9.7 %while.29 = (s32[]{:T(128)}, f32[128,8,64]{0,2,1:T(8,128)}, s32[]{:T(128)}, bf16[1024,512]{0,1:T(8,128)(2,1)S(1)}, bf16[128,8,64]{0,2,1:T(8,128)(2,1)S(1)}, /*in...) while((s32[]{:T(128)}, f32[128,8,64]{0,2,1:T(8,128)}, ...), condition=%wide.region_14.15_spmd.clone, body=%wide.region_13.14_spmd.clone.sunk | while | flops 415433856 | bytes 11543673 | solution.py:204
  126.5 2.8 fusion.121
  130.0 6.2 %fusion.122 = f32[128,8,64]{0,2,1:T(8,128)} fusion(f32[128,8,64]{0,2,1:T(8,128)} %get-tuple-element.462, bf16[1024,8,64]{0,2,1:T(8,128)(2,1)} %bitcast.118, f32[8,128,1024]{2,1,0:T(8,128)} %fusion.121, bf16[128,8,64]{0,2,1:T(8,128)(2,1)} %get-tuple-element.477, pred[128,1024]{1,0:T(8,128)(4,1)} %broadcast_compare_fusion.7), kind=kOutput, calls=%fused_computation.40.clone.1 | convolution fusion | flops 281083904 | bytes 6029312 | tf_op jit(solution)/shard_map/while/body/hqk,khd->qhd/dot_general | solution.py:199
  136.2 1.8 copy.59
  138.0 2.2 fusion.71
  140.3 21.0 %all-gather.9.cloned.1.call-done = bf16[1024,512]{1,0:T(8,128)(2,1)} async-done(((bf16[128,512]{1,0:T(8,128)(2,1)}), bf16[1024,512]{1,0:T(8,128)(2,1)}) %all-gather.9.cloned.1.call-update) | async-done | bytes 1048592 | tf_op jit(solution)/shard_map/all_gather | solution.py:209
  162.6 22.0 %conditional.1 = (f32[128,8,64]{0,2,1:T(8,128)}, f32[128,8,64]{0,2,1:T(8,128)}) conditional(s32[]{:T(128)} %convert_element_type.78, f32[128,8,64]{0,2,1:T(8,128)} %broadcast.362, (s32[128]{0:T(128)}, s32[1024]{0:T(1024)}, bf16[1024,512]{1,0:T(8,128)(2,1)}, bf16[128,512]{1,0:T(8,128)(2,1)}, bf16[1024,512]{1,0:T(8,128)(2,1)}, ...), branch_computations={%region_11.12_spmd, %region_12.13_spmd} | conditional | flops 557056000 | bytes 24253000 | solution.py:241
  162.6 1.5 copy.53
  164.1 1.7 copy.54
  165.8 3.7 fusion.69
  169.5 2.3 copy.51
  171.8 1.5 broadcast_compare_fusion
  174.1 5.9 %fusion.9 = f32[128,8,64]{0,2,1:T(8,128)} fusion(f32[128,8,64]{0,2,1:T(8,128)} %get-tuple-element.132, bf16[1024,8,64]{0,2,1:T(8,128)(2,1)S(1)} %bitcast.116, f32[8,1024,128]{2,1,0:T(8,128)} %fusion.69, bf16[1024,8,64]{0,2,1:T(8,128)(2,1)} %bitcast.119, bf16[128,8,64]{0,2,1:T(8,128)(2,1)} %bitcast.126, pred[1024,128]{1,0:T(8,128)(4,1)} %broadcast_compare_fusion), kind=kOutput, calls=%fused_computation.19 | convolution fusion | flops 281083904 | bytes 7077888 | tf_op jit(solution)/shard_map/while/body/eval_jaxpr/cond/branch_1_fun/hqk,qhd->khd/dot_general | solution.py:233
  180.0 4.6 %fusion.8 = f32[128,8,64]{0,2,1:T(8,128)} fusion(f32[128,8,64]{0,2,1:T(8,128)} %get-tuple-element.132, bf16[1024,8,64]{0,2,1:T(8,128)(2,1)} %bitcast.120, f32[8,1024,128]{2,1,0:T(8,128)} %fusion.69, pred[1024,128]{1,0:T(8,128)(4,1)S(1)} %copy-done.13), kind=kOutput, calls=%fused_computation.18 | convolution fusion | flops 141623296 | bytes 5898240 | tf_op jit(solution)/shard_map/while/body/eval_jaxpr/cond/branch_1_fun/hqk,qhd->khd/dot_general | solution.py:236
  184.6 1.1 copy.58
  185.7 1.1 copy.60
  186.8 1.8 fusion.30
  188.5 3.6 fusion.61
  193.3 1.2 fusion.46
  196.6 4.7 %all-to-all-start.4 = ((f32[32,10,128]{2,1,0:T(8,128)}), f32[32,10,128]{2,1,0:T(8,128)}, u32[]{:S(2)}, u32[]{:S(2)}) async-start(f32[32,10,128]{2,1,0:T(8,128)} %reshape.392), calls=%async_computation.4 | async-start | bytes 524288 | tf_op jit(solution)/shard_map/all_to_all | solution.py:287
  201.3 1.4 scatter_custom_fusion.1
  203.7 11.2 %all-to-all-done.4 = f32[32,10,128]{2,1,0:T(8,128)} async-done(((f32[32,10,128]{2,1,0:T(8,128)}), f32[32,10,128]{2,1,0:T(8,128)}, u32[]{:S(2)}, u32[]{:S(2)}) %all-to-all-start.4) | async-done | bytes 163872 | tf_op jit(solution)/shard_map/all_to_all | solution.py:287
  214.9 2.7 all-to-all-start.3
  219.0 2.0 fusion.28
  221.9 2.6 scatter_custom_fusion.4
  224.5 30.8 %all-to-all-done.3 = f32[32,10,512]{2,1,0:T(8,128)S(1)} async-done(((f32[32,10,512]{2,1,0:T(8,128)}), f32[32,10,512]{2,1,0:T(8,128)S(1)}, u32[]{:S(2)}, u32[]{:S(2)}) %all-to-all-start.3) | async-done | bytes 655392 | tf_op jit(solution)/shard_map/all_to_all | solution.py:286
  256.2 4.0 %scatter_custom_fusion.2 = f32[512,512]{1,0:T(8,128)} fusion(s32[320]{0:T(512)S(1)} %get-tuple-element.272, f32[320,512]{1,0:T(8,128)} %reshape.446, f32[]{:T(128)} %constant.57.clone.1), kind=kCustom, calls=%fused_computation.61 | custom fusion | flops 163840 | bytes 1049088 | tf_op jit(solution)/shard_map/scatter-add | solution.py:294
  260.2 111.1 %all-reduce.3.cloned.1.call-done = (f32[128,512]{1,0:T(8,128)}, f32[512,2048]{1,0:T(8,128)}, f32[512,512]{1,0:T(8,128)}) async-done(((f32[128,512]{1,0:T(8,128)}, f32[512,2048]{1,0:T(8,128)}, f32[512,512]{1,0:T(8,128)}), (f32[128,512]{1,0:T(8,128)}, f32[512,2048]{1,0:T(8,128)}, f32[512,512]{1,0:T(8,128)})) %all-reduce.3.cloned.1.call-update) | async-done | bytes 5505040 | tf_op jit(solution)/shard_map/psum | solution.py:261
  371.3 4.9 %broadcast_multiply_fusion = f32[512,2048]{1,0:T(8,128)} fusion(f32[512,2048]{1,0:T(8,128)} %get-tuple-element.304), kind=kLoop, calls=%fused_computation.47 | loop fusion | flops 1048576 | bytes 8388608 | tf_op jit(solution)/shard_map/mul | solution.py:306
  (119 shorter events, 29.8 us)
Async XLA Ops:
  7.2 52.9 %copy-start = (bf16[512,2048]{1,0:T(8,128)(2,1)S(1)}, bf16[512,2048]{1,0:T(8,128)(2,1)}, u32[]{:S(2)}) copy-start(bf16[512,2048]{1,0:T(8,128)(2,1)} %param.19) | copy-start | bytes 6291460
  7.2 25.1 %copy-start.1 = (bf16[512,512]{1,0:T(8,128)(2,1)S(1)}, bf16[512,512]{1,0:T(8,128)(2,1)}, u32[]{:S(2)}) copy-start(bf16[512,512]{1,0:T(8,128)(2,1)} %param.16) | copy-start | bytes 1572868
  8.9 34.2 %copy-start.21 = (s32[128]{0:T(128)}, s32[128]{0:T(128)S(1)}, u32[]{:S(2)}) copy-start(s32[128]{0:T(128)S(1)} %fusion.57) | copy-start | bytes 1540
  10.7 14.4 %all-to-all-start = ((s32[32,1,10]{2,1,0:T(1,128)}), s32[32,1,10]{2,1,0:T(1,128)S(1)}, u32[]{:S(2)}, u32[]{:S(2)}) async-start(s32[32,1,10]{2,1,0:T(1,128)} %bitcast.9), calls=%async_computation | async-start | bytes 32768 | tf_op jit(solution)/shard_map/all_to_all | solution.py:92
  28.8 14.3 %copy-start.22 = (s32[128]{0:T(128)S(1)}, s32[128]{0:T(128)}, u32[]{:S(2)}) copy-start(s32[128]{0:T(128)} %param.15) | copy-start | bytes 1540
  29.6 10.8 %all-to-all-start.2 = ((bf16[32,10,128]{2,1,0:T(8,128)(2,1)}), bf16[32,10,128]{2,1,0:T(8,128)(2,1)S(1)}, u32[]{:S(2)}, u32[]{:S(2)}) async-start(bf16[32,10,128]{2,1,0:T(8,128)(2,1)} %broadcast_select_fusion.1), calls=%async_computation.2 | async-start | bytes 262144 | tf_op jit(solution)/shard_map/all_to_all | solution.py:106
  32.3 27.3 %copy-start.8 = (bf16[128,512]{1,0:T(8,128)(2,1)S(1)}, bf16[128,512]{1,0:T(8,128)(2,1)}, u32[]{:S(2)}) copy-start(bf16[128,512]{1,0:T(8,128)(2,1)} %param.18) | copy-start | bytes 393220
  40.4 18.2 %all-to-all-start.1 = ((bf16[32,10,512]{2,1,0:T(8,128)(2,1)}), bf16[32,10,512]{2,1,0:T(8,128)(2,1)S(1)}, u32[]{:S(2)}, u32[]{:S(2)}) async-start(bf16[32,10,512]{2,1,0:T(8,128)(2,1)} %broadcast_select_fusion), calls=%async_computation.1 | async-start | bytes 1048576 | tf_op jit(solution)/shard_map/all_to_all | solution.py:105
  43.0 41.9 %all-gather.5.cloned.1.call-start = ((), (), s32[]{:S(2)}) async-start(), calls=%async_computation.5 | async-start | bytes 1179648 | tf_op jit(solution)/shard_map/all_gather | solution.py:126
  43.7 16.2 %copy-start.18 = (pred[128]{0:T(512)(128)(4,1)}, pred[128]{0:T(512)(128)(4,1)S(1)}, u32[]{:S(2)}) copy-start(pred[128]{0:T(512)(128)(4,1)S(1)} %get-tuple-element.317) | copy-start | bytes 388
  44.4 17.2 %copy-start.10 = (bf16[128,128]{1,0:T(8,128)(2,1)}, bf16[128,128]{1,0:T(8,128)(2,1)S(1)}, u32[]{:S(2)}) copy-start(bf16[128,128]{1,0:T(8,128)(2,1)S(1)} %gather_fusion.3) | copy-start | bytes 98308
  59.9 27.3 %copy-start.14 = (f32[128]{0:T(128)}, f32[128]{0:T(128)S(1)}, u32[]{:S(2)}) copy-start(f32[128]{0:T(128)S(1)} %broadcast_multiply_fusion.8) | copy-start | bytes 1540
  60.1 27.1 %copy-start.16 = (f32[128]{0:T(128)}, f32[128]{0:T(128)S(1)}, u32[]{:S(2)}) copy-start(f32[128]{0:T(128)S(1)} %add_rsqrt_fusion.1) | copy-start | bytes 1540
  61.6 0.8 copy-start.7
  63.1 3.4 copy-start.4
  63.1 47.7 %all-gather.7.cloned.1.call-start = ((), (), s32[]{:S(2)}) async-start(), calls=%async_computation.6 | async-start | bytes 1179648 | tf_op jit(solution)/shard_map/all_gather | solution.py:127
  63.9 76.4 %all-gather.11.cloned.1.call-start = ((), (), s32[]{:S(2)}) async-start(), calls=%async_computation.8 | async-start | bytes 1179648 | tf_op jit(solution)/shard_map/all_gather | solution.py:208
  66.5 94.7 %all-gather.9.cloned.1.call-start = ((), (), s32[]{:S(2)}) async-start(), calls=%async_computation.7 | async-start | bytes 1179648 | tf_op jit(solution)/shard_map/all_gather | solution.py:209
  125.7 245.6 %all-reduce.3.cloned.1.call-start = ((), (), s32[]{:S(2)}) async-start(), calls=%async_computation.9 | async-start | bytes 11010048 | tf_op jit(solution)/shard_map/psum | solution.py:261
  164.1 9.2 %copy-start.3 = (bf16[128,512]{1,0:T(8,128)(2,1)S(1)}, bf16[128,512]{1,0:T(8,128)(2,1)}, u32[]{:S(2)}) copy-start(bf16[128,512]{1,0:T(8,128)(2,1)} %get-tuple-element.255) | copy-start | bytes 393220 | tf_op jit(solution)/shard_map/while/body/eval_jaxpr/cond
  174.1 5.9 %copy-start.13 = (pred[1024,128]{1,0:T(8,128)(4,1)S(1)}, pred[1024,128]{1,0:T(8,128)(4,1)}, u32[]{:S(2)}) copy-start(pred[1024,128]{1,0:T(8,128)(4,1)} %broadcast_compare_fusion) | copy-start | bytes 393220 | tf_op jit(solution)/shard_map/while/body/eval_jaxpr/cond
  185.6 6.5 %copy-start.15 = (f32[128]{0:T(128)S(1)}, f32[128]{0:T(128)}, u32[]{:S(2)}) copy-start(f32[128]{0:T(128)} %copy-done.14) | copy-start | bytes 1540
  185.7 6.4 %copy-start.17 = (f32[128]{0:T(128)S(1)}, f32[128]{0:T(128)}, u32[]{:S(2)}) copy-start(f32[128]{0:T(128)} %copy-done.16) | copy-start | bytes 1540
  188.5 4.5 %copy-start.2 = (bf16[128,512]{1,0:T(8,128)(2,1)S(1)}, bf16[128,512]{1,0:T(8,128)(2,1)}, u32[]{:S(2)}) copy-start(bf16[128,512]{1,0:T(8,128)(2,1)} %param.21) | copy-start | bytes 393220
  188.5 4.7 %copy-start.11 = (bf16[128,128]{1,0:T(8,128)(2,1)S(1)}, bf16[128,128]{1,0:T(8,128)(2,1)}, u32[]{:S(2)}) copy-start(bf16[128,128]{1,0:T(8,128)(2,1)} %copy-done.10) | copy-start | bytes 98308
  188.5 4.7 %copy-start.20 = (pred[128]{0:T(512)(128)(4,1)S(1)}, pred[128]{0:T(512)(128)(4,1)}, u32[]{:S(2)}) copy-start(pred[128]{0:T(512)(128)(4,1)} %get-tuple-element.316) | copy-start | bytes 388
  193.0 1.5 copy-start.9
  193.1 8.2 %copy-start.19 = (pred[128]{0:T(512)(128)(4,1)S(1)}, pred[128]{0:T(512)(128)(4,1)}, u32[]{:S(2)}) copy-start(pred[128]{0:T(512)(128)(4,1)} %copy-done.18) | copy-start | bytes 388
  194.5 24.5 %copy-start.5 = (bf16[128,512]{1,0:T(8,128)(2,1)S(1)}, bf16[128,512]{1,0:T(8,128)(2,1)}, u32[]{:S(2)}) copy-start(bf16[128,512]{1,0:T(8,128)(2,1)} %get-tuple-element.307) | copy-start | bytes 393220
  196.6 18.4 %all-to-all-start.4 = ((f32[32,10,128]{2,1,0:T(8,128)}), f32[32,10,128]{2,1,0:T(8,128)}, u32[]{:S(2)}, u32[]{:S(2)}) async-start(f32[32,10,128]{2,1,0:T(8,128)} %reshape.392), calls=%async_computation.4 | async-start | bytes 524288 | tf_op jit(solution)/shard_map/all_to_all | solution.py:287
  214.9 40.4 %all-to-all-start.3 = ((f32[32,10,512]{2,1,0:T(8,128)}), f32[32,10,512]{2,1,0:T(8,128)S(1)}, u32[]{:S(2)}, u32[]{:S(2)}) async-start(f32[32,10,512]{2,1,0:T(8,128)} %reshape.390), calls=%async_computation.3 | async-start | bytes 2097152 | tf_op jit(solution)/shard_map/all_to_all | solution.py:286
  371.3 4.9 %copy-start.6 = (f32[512,512]{1,0:T(8,128)S(1)}, f32[512,512]{1,0:T(8,128)}, u32[]{:S(2)}) copy-start(f32[512,512]{1,0:T(8,128)} %get-tuple-element.305) | copy-start | bytes 3145732
  371.3 6.0 %copy-start.12 = (f32[128,512]{1,0:T(8,128)S(1)}, f32[128,512]{1,0:T(8,128)}, u32[]{:S(2)}) copy-start(f32[128,512]{1,0:T(8,128)} %get-tuple-element.303) | copy-start | bytes 786436
Sparse Core Ops, SparseCore 0:
  63.3 21.6 all-gather.4
  87.4 23.3 all-gather.6
  112.7 23.3 all-gather.10
  137.9 23.3 all-gather.8
  194.6 176.6 all-reduce.2
where the time goes:
time: 386 us; the launch traced here: 385 us
  waiting for transfers between devices  243 us (63%)
  matrix products  41.7 us (11%)
  local copies, waits for them, and re-layouts  35.9 us (9%)
  other arithmetic  28.9 us (7%)
  starting transfers between devices  20.1 us (5%)
  between operations  14.9 us (4%)
    psum x1, waiting for transfers between devices, local(): lax.psum((joined_local, output_local, projection_local), ('dp', 'cp'))  111 us
    all_to_all x1, waiting for transfers between devices, local(): lax.all_to_all(hot_buffer, ('dp', 'cp'), split_axis=0, concat_axis=0, til...  30.8 us
    all_gather x1, waiting for transfers between devices, local(): lax.all_gather(value_rows, 'cp', axis=0, tiled=True)  23.6 us
    all_gather x1, waiting for transfers between devices, local(): delta_piece = lax.all_gather(delta_attended, 'cp', axis=0, tiled=True)  21 us
    all_gather x1, waiting for transfers between devices, local(): lax.all_gather(key_rows, 'cp', axis=0, tiled=True)  18.3 us
    all_to_all x1, waiting for transfers between devices, local(): lax.all_to_all(hot_pick, ('dp', 'cp'), split_axis=0, concat_axis=0, tiled...  14.2 us
    all_to_all x1, waiting for transfers between devices, local(): lax.all_to_all(cold_buffer, ('dp', 'cp'), split_axis=0, concat_axis=0, ti...  11.2 us
    another operation x8, local copies, waits for them, and re-layouts  8.38 us
  transfers between devices with their start and end apart: 10, of which 9 were waited for; matrix products, arithmetic and copies ran while one was open for 14% of the time, Pallas kernels for 0%

commit v1 on v0

--- a/solution.py
+++ b/solution.py
@@ -7,6 +7,11 @@
 HEADS = 8
 EPSILON = 1e-05
 block_limit = 1024
+
+
+def axis_by_axis(array, axis_one, axis_two):
+    half = lax.psum(array, axis_one)
+    return lax.psum(half, axis_two)
 
 
 def silu_slope(values):
@@ -258,8 +263,8 @@
     joined_local = jnp.dot(normed_low.T, delta_hidden, preferred_element_type=jnp.float32)
     output_local = jnp.dot(gated.T, cotangent, preferred_element_type=jnp.float32)
     projection_local = jnp.dot(cold_float.T, delta_embed, precision=lax.Precision.HIGHEST)
-    joined_sum, output_sum, projection_sum = lax.psum(
-        (joined_local, output_local, projection_local), ("dp", "cp")
+    joined_sum, output_sum, projection_sum = axis_by_axis(
+        (joined_local, output_local, projection_local), "cp", "dp"
     )
     norm_scale = (tokens_here * devices) ** (-0.5)
     cold_event = jnp.where(

time: 386 us -> 532 us (1.38)
  waiting for transfers between devices: 243 us -> 385 us
    psum x1 -> x2, waiting for transfers between devices: 111 us -> 235 us  [the longest x1 140 us: axis_by_axis(): return lax.psum(half, axis_two)]
    all_to_all x1, waiting for transfers between devices: 30.8 us -> 45.8 us  [local(): lax.all_to_all(hot_buffer, ('dp', 'cp'), split_axis=0, concat_axis=0, til...]
  transfers between devices with their start and end apart: 10 -> 11, of which waited for: 9 -> 10; matrix products, arithmetic and copies ran while one was open for 14% -> 10% of each run, Pallas kernels for 0% -> 0%
where the time goes in v1:
time: 532 us; the launch traced here: 531 us
  waiting for transfers between devices  385 us (72%)
  matrix products  41.7 us (8%)
  local copies, waits for them, and re-layouts  35.8 us (7%)
  other arithmetic  28.9 us (5%)
  starting transfers between devices  24.6 us (5%)
  between operations  15.3 us (3%)
    psum x1, waiting for transfers between devices, axis_by_axis(): return lax.psum(half, axis_two)  140 us
    psum x1, waiting for transfers between devices, axis_by_axis(): half = lax.psum(array, axis_one)  95.4 us
    all_to_all x1, waiting for transfers between devices, local(): lax.all_to_all(hot_buffer, ('dp', 'cp'), split_axis=0, concat_axis=0, til...  45.8 us
    all_gather x1, waiting for transfers between devices, local(): lax.all_gather(value_rows, 'cp', axis=0, tiled=True)  23.6 us
    all_gather x1, waiting for transfers between devices, local(): delta_piece = lax.all_gather(delta_attended, 'cp', axis=0, tiled=True)  21 us
    all_gather x1, waiting for transfers between devices, local(): lax.all_gather(key_rows, 'cp', axis=0, tiled=True)  18.4 us
    all_to_all x1, waiting for transfers between devices, local(): lax.all_to_all(hot_pick, ('dp', 'cp'), split_axis=0, concat_axis=0, tiled...  14.2 us
    all_to_all x1, waiting for transfers between devices, local(): lax.all_to_all(cold_buffer, ('dp', 'cp'), split_axis=0, concat_axis=0, ti...  13.7 us
  transfers between devices with their start and end apart: 11, of which 10 were waited for; matrix products, arithmetic and copies ran while one was open for 10% of the time, Pallas kernels for 0%

profile of v1, /device:TPU:0, one launch (start us, length us, event | category | flops | bytes accessed | tf_op | source)
XLA Modules:
  0.0 530.9 jit_solution(9245627003133395092)
XLA Ops:
  8.9 1.1 scatter_custom_fusion
  10.7 7.3 %all-to-all-start = ((s32[32,1,10]{2,1,0:T(1,128)}), s32[32,1,10]{2,1,0:T(1,128)S(1)}, u32[]{:S(2)}, u32[]{:S(2)}) async-start(s32[32,1,10]{2,1,0:T(1,128)} %bitcast.9), calls=%async_computation | async-start | bytes 32768 | tf_op jit(solution)/shard_map/all_to_all | solution.py:97
  18.0 7.1 %all-to-all-done = s32[32,1,10]{2,1,0:T(1,128)S(1)} async-done(((s32[32,1,10]{2,1,0:T(1,128)}), s32[32,1,10]{2,1,0:T(1,128)S(1)}, u32[]{:S(2)}, u32[]{:S(2)}) %all-to-all-start) | async-done | bytes 1312 | tf_op jit(solution)/shard_map/all_to_all | solution.py:97
  26.5 2.2 gather_fusion.2
  29.6 2.6 all-to-all-start.2
  32.3 2.0 gather_fusion
  35.4 5.0 all-to-all-done.2
  40.4 2.6 all-to-all-start.1
  44.4 14.2 %all-to-all-done.1 = bf16[32,10,512]{2,1,0:T(8,128)(2,1)S(1)} async-done(((bf16[32,10,512]{2,1,0:T(8,128)(2,1)}), bf16[32,10,512]{2,1,0:T(8,128)(2,1)S(1)}, u32[]{:S(2)}, u32[]{:S(2)}) %all-to-all-start.1) | async-done | bytes 327712 | tf_op jit(solution)/shard_map/all_to_all | solution.py:110
  60.1 1.5 multiply_convert_fusion
  66.6 18.4 %all-gather.5.cloned.1.call-done = bf16[1024,512]{1,0:T(8,128)(2,1)} async-done(((bf16[128,512]{1,0:T(8,128)(2,1)}), bf16[1024,512]{1,0:T(8,128)(2,1)}) %all-gather.5.cloned.1.call-update) | async-done | bytes 1048592 | tf_op jit(solution)/shard_map/all_gather | solution.py:131
  85.0 2.3 copy.48
  87.2 23.6 %all-gather.7.cloned.1.call-done = bf16[1024,512]{1,0:T(8,128)(2,1)} async-done(((bf16[128,512]{1,0:T(8,128)(2,1)}), bf16[1024,512]{1,0:T(8,128)(2,1)}) %all-gather.7.cloned.1.call-update) | async-done | bytes 1048592 | tf_op jit(solution)/shard_map/all_gather | solution.py:132
  110.8 1.5 copy.49
  113.0 4.2 while.28
  113.2 4.0 fusion.115
  118.3 1.8 copy.50
  121.1 1.6 fusion.45
  122.7 1.9 multiply_convert_fusion.1
  126.5 9.7 %while.29 = (s32[]{:T(128)}, f32[128,8,64]{0,2,1:T(8,128)}, s32[]{:T(128)}, bf16[1024,512]{0,1:T(8,128)(2,1)S(1)}, bf16[128,8,64]{0,2,1:T(8,128)(2,1)S(1)}, /*in...) while((s32[]{:T(128)}, f32[128,8,64]{0,2,1:T(8,128)}, ...), condition=%wide.region_14.15_spmd.clone, body=%wide.region_13.14_spmd.clone.sunk | while | flops 415433856 | bytes 11543673 | solution.py:209
  126.5 2.8 fusion.121
  130.0 6.2 %fusion.122 = f32[128,8,64]{0,2,1:T(8,128)} fusion(f32[128,8,64]{0,2,1:T(8,128)} %get-tuple-element.465, bf16[1024,8,64]{0,2,1:T(8,128)(2,1)} %bitcast.118, f32[8,128,1024]{2,1,0:T(8,128)} %fusion.121, bf16[128,8,64]{0,2,1:T(8,128)(2,1)} %get-tuple-element.480, pred[128,1024]{1,0:T(8,128)(4,1)} %broadcast_compare_fusion.7), kind=kOutput, calls=%fused_computation.40.clone.1 | convolution fusion | flops 281083904 | bytes 6029312 | tf_op jit(solution)/shard_map/while/body/hqk,khd->qhd/dot_general | solution.py:204
  136.2 1.8 copy.59
  138.0 2.3 fusion.71
  140.2 21.0 %all-gather.9.cloned.1.call-done = bf16[1024,512]{1,0:T(8,128)(2,1)} async-done(((bf16[128,512]{1,0:T(8,128)(2,1)}), bf16[1024,512]{1,0:T(8,128)(2,1)}) %all-gather.9.cloned.1.call-update) | async-done | bytes 1048592 | tf_op jit(solution)/shard_map/all_gather | solution.py:214
  162.6 22.0 %conditional.1 = (f32[128,8,64]{0,2,1:T(8,128)}, f32[128,8,64]{0,2,1:T(8,128)}) conditional(s32[]{:T(128)} %convert_element_type.78, f32[128,8,64]{0,2,1:T(8,128)} %broadcast.362, (s32[128]{0:T(128)}, s32[1024]{0:T(1024)}, bf16[1024,512]{1,0:T(8,128)(2,1)}, bf16[128,512]{1,0:T(8,128)(2,1)}, bf16[1024,512]{1,0:T(8,128)(2,1)}, ...), branch_computations={%region_11.12_spmd, %region_12.13_spmd} | conditional | flops 557056000 | bytes 24253000 | solution.py:246
  162.6 1.5 copy.53
  164.1 1.7 copy.54
  165.8 3.7 fusion.69
  169.5 2.3 copy.51
  171.8 1.5 broadcast_compare_fusion
  174.1 5.9 %fusion.9 = f32[128,8,64]{0,2,1:T(8,128)} fusion(f32[128,8,64]{0,2,1:T(8,128)} %get-tuple-element.132, bf16[1024,8,64]{0,2,1:T(8,128)(2,1)S(1)} %bitcast.116, f32[8,1024,128]{2,1,0:T(8,128)} %fusion.69, bf16[1024,8,64]{0,2,1:T(8,128)(2,1)} %bitcast.119, bf16[128,8,64]{0,2,1:T(8,128)(2,1)} %bitcast.126, pred[1024,128]{1,0:T(8,128)(4,1)} %broadcast_compare_fusion), kind=kOutput, calls=%fused_computation.19 | convolution fusion | flops 281083904 | bytes 7077888 | tf_op jit(solution)/shard_map/while/body/eval_jaxpr/cond/branch_1_fun/hqk,qhd->khd/dot_general | solution.py:238
  180.0 4.6 fusion.8
  185.7 1.1 copy.60
  186.8 1.8 fusion.30
  188.6 3.6 fusion.61
  193.2 1.2 fusion.46
  194.5 95.4 %all-reduce.5.cloned.1.call-done = (f32[128,512]{1,0:T(8,128)}, f32[512,2048]{1,0:T(8,128)}, f32[512,512]{1,0:T(8,128)}) async-done(((f32[128,512]{1,0:T(8,128)}, f32[512,2048]{1,0:T(8,128)}, f32[512,512]{1,0:T(8,128)}), (f32[128,512]{1,0:T(8,128)}, f32[512,2048]{1,0:T(8,128)}, f32[512,512]{1,0:T(8,128)})) %all-reduce.5.cloned.1.call-update) | async-done | bytes 5505040 | tf_op jit(solution)/shard_map/psum | solution.py:13
  292.1 4.8 all-to-all-start.4
  296.9 1.4 scatter_custom_fusion.1
  299.3 13.7 %all-to-all-done.4 = f32[32,10,128]{2,1,0:T(8,128)} async-done(((f32[32,10,128]{2,1,0:T(8,128)}), f32[32,10,128]{2,1,0:T(8,128)}, u32[]{:S(2)}, u32[]{:S(2)}) %all-to-all-start.4) | async-done | bytes 163872 | tf_op jit(solution)/shard_map/all_to_all | solution.py:292
  313.1 7.0 %all-to-all-start.3 = ((f32[32,10,512]{2,1,0:T(8,128)}), f32[32,10,512]{2,1,0:T(8,128)S(1)}, u32[]{:S(2)}, u32[]{:S(2)}) async-start(f32[32,10,512]{2,1,0:T(8,128)} %reshape.390), calls=%async_computation.3 | async-start | bytes 2097152 | tf_op jit(solution)/shard_map/all_to_all | solution.py:291
  321.4 1.9 fusion.28
  324.4 2.6 scatter_custom_fusion.4
  327.0 45.8 %all-to-all-done.3 = f32[32,10,512]{2,1,0:T(8,128)S(1)} async-done(((f32[32,10,512]{2,1,0:T(8,128)}), f32[32,10,512]{2,1,0:T(8,128)S(1)}, u32[]{:S(2)}, u32[]{:S(2)}) %all-to-all-start.3) | async-done | bytes 655392 | tf_op jit(solution)/shard_map/all_to_all | solution.py:291
  373.7 4.0 scatter_custom_fusion.2
  377.8 139.6 %all-reduce.7.cloned.1.call-done = (f32[128,512]{1,0:T(8,128)}, f32[512,2048]{1,0:T(8,128)}, f32[512,512]{1,0:T(8,128)}) async-done(((f32[128,512]{1,0:T(8,128)}, f32[512,2048]{1,0:T(8,128)}, f32[512,512]{1,0:T(8,128)}), (f32[128,512]{1,0:T(8,128)}, f32[512,2048]{1,0:T(8,128)}, f32[512,512]{1,0:T(8,128)})) %all-reduce.7.cloned.1.call-update) | async-done | bytes 5505040 | tf_op jit(solution)/shard_map/psum | solution.py:14
  517.3 4.9 broadcast_multiply_fusion
  (122 shorter events, 30.9 us)
Async XLA Ops:
  7.2 52.9 %copy-start = (bf16[512,2048]{1,0:T(8,128)(2,1)S(1)}, bf16[512,2048]{1,0:T(8,128)(2,1)}, u32[]{:S(2)}) copy-start(bf16[512,2048]{1,0:T(8,128)(2,1)} %param.19) | copy-start | bytes 6291460
  7.2 25.1 %copy-start.1 = (bf16[512,512]{1,0:T(8,128)(2,1)S(1)}, bf16[512,512]{1,0:T(8,128)(2,1)}, u32[]{:S(2)}) copy-start(bf16[512,512]{1,0:T(8,128)(2,1)} %param.16) | copy-start | bytes 1572868
  8.9 34.2 %copy-start.21 = (s32[128]{0:T(128)}, s32[128]{0:T(128)S(1)}, u32[]{:S(2)}) copy-start(s32[128]{0:T(128)S(1)} %fusion.57) | copy-start | bytes 1540
  10.7 14.4 %all-to-all-start = ((s32[32,1,10]{2,1,0:T(1,128)}), s32[32,1,10]{2,1,0:T(1,128)S(1)}, u32[]{:S(2)}, u32[]{:S(2)}) async-start(s32[32,1,10]{2,1,0:T(1,128)} %bitcast.9), calls=%async_computation | async-start | bytes 32768 | tf_op jit(solution)/shard_map/all_to_all | solution.py:97
  28.8 14.3 %copy-start.22 = (s32[128]{0:T(128)S(1)}, s32[128]{0:T(128)}, u32[]{:S(2)}) copy-start(s32[128]{0:T(128)} %param.15) | copy-start | bytes 1540
  29.6 10.8 %all-to-all-start.2 = ((bf16[32,10,128]{2,1,0:T(8,128)(2,1)}), bf16[32,10,128]{2,1,0:T(8,128)(2,1)S(1)}, u32[]{:S(2)}, u32[]{:S(2)}) async-start(bf16[32,10,128]{2,1,0:T(8,128)(2,1)} %broadcast_select_fusion.1), calls=%async_computation.2 | async-start | bytes 262144 | tf_op jit(solution)/shard_map/all_to_all | solution.py:111
  32.3 27.3 %copy-start.8 = (bf16[128,512]{1,0:T(8,128)(2,1)S(1)}, bf16[128,512]{1,0:T(8,128)(2,1)}, u32[]{:S(2)}) copy-start(bf16[128,512]{1,0:T(8,128)(2,1)} %param.18) | copy-start | bytes 393220
  40.4 18.2 %all-to-all-start.1 = ((bf16[32,10,512]{2,1,0:T(8,128)(2,1)}), bf16[32,10,512]{2,1,0:T(8,128)(2,1)S(1)}, u32[]{:S(2)}, u32[]{:S(2)}) async-start(bf16[32,10,512]{2,1,0:T(8,128)(2,1)} %broadcast_select_fusion), calls=%async_computation.1 | async-start | bytes 1048576 | tf_op jit(solution)/shard_map/all_to_all | solution.py:110
  43.0 41.9 %all-gather.5.cloned.1.call-start = ((), (), s32[]{:S(2)}) async-start(), calls=%async_computation.5 | async-start | bytes 1179648 | tf_op jit(solution)/shard_map/all_gather | solution.py:131
  43.7 16.2 %copy-start.18 = (pred[128]{0:T(512)(128)(4,1)}, pred[128]{0:T(512)(128)(4,1)S(1)}, u32[]{:S(2)}) copy-start(pred[128]{0:T(512)(128)(4,1)S(1)} %get-tuple-element.320) | copy-start | bytes 388
  44.4 17.2 %copy-start.10 = (bf16[128,128]{1,0:T(8,128)(2,1)}, bf16[128,128]{1,0:T(8,128)(2,1)S(1)}, u32[]{:S(2)}) copy-start(bf16[128,128]{1,0:T(8,128)(2,1)S(1)} %gather_fusion.3) | copy-start | bytes 98308
  59.9 27.3 %copy-start.14 = (f32[128]{0:T(128)}, f32[128]{0:T(128)S(1)}, u32[]{:S(2)}) copy-start(f32[128]{0:T(128)S(1)} %broadcast_multiply_fusion.8) | copy-start | bytes 1540
  60.1 27.1 %copy-start.16 = (f32[128]{0:T(128)}, f32[128]{0:T(128)S(1)}, u32[]{:S(2)}) copy-start(f32[128]{0:T(128)S(1)} %add_rsqrt_fusion.1) | copy-start | bytes 1540
  61.6 0.8 copy-start.7
  63.1 3.4 copy-start.4
  63.2 47.7 %all-gather.7.cloned.1.call-start = ((), (), s32[]{:S(2)}) async-start(), calls=%async_computation.6 | async-start | bytes 1179648 | tf_op jit(solution)/shard_map/all_gather | solution.py:132
  63.9 76.3 %all-gather.11.cloned.1.call-start = ((), (), s32[]{:S(2)}) async-start(), calls=%async_computation.8 | async-start | bytes 1179648 | tf_op jit(solution)/shard_map/all_gather | solution.py:213
  66.6 94.7 %all-gather.9.cloned.1.call-start = ((), (), s32[]{:S(2)}) async-start(), calls=%async_computation.7 | async-start | bytes 1179648 | tf_op jit(solution)/shard_map/all_gather | solution.py:214
  125.7 164.3 %all-reduce.5.cloned.1.call-start = ((), (), s32[]{:S(2)}) async-start(), calls=%async_computation.9 | async-start | bytes 11010048 | tf_op jit(solution)/shard_map/psum | solution.py:13
  164.1 9.2 %copy-start.3 = (bf16[128,512]{1,0:T(8,128)(2,1)S(1)}, bf16[128,512]{1,0:T(8,128)(2,1)}, u32[]{:S(2)}) copy-start(bf16[128,512]{1,0:T(8,128)(2,1)} %get-tuple-element.255) | copy-start | bytes 393220 | tf_op jit(solution)/shard_map/while/body/eval_jaxpr/cond
  174.1 5.9 %copy-start.13 = (pred[1024,128]{1,0:T(8,128)(4,1)S(1)}, pred[1024,128]{1,0:T(8,128)(4,1)}, u32[]{:S(2)}) copy-start(pred[1024,128]{1,0:T(8,128)(4,1)} %broadcast_compare_fusion) | copy-start | bytes 393220 | tf_op jit(solution)/shard_map/while/body/eval_jaxpr/cond
  185.7 6.5 %copy-start.15 = (f32[128]{0:T(128)S(1)}, f32[128]{0:T(128)}, u32[]{:S(2)}) copy-start(f32[128]{0:T(128)} %copy-done.14) | copy-start | bytes 1540
  185.7 6.4 %copy-start.17 = (f32[128]{0:T(128)S(1)}, f32[128]{0:T(128)}, u32[]{:S(2)}) copy-start(f32[128]{0:T(128)} %copy-done.16) | copy-start | bytes 1540
  188.5 4.5 copy-start.2
  188.5 4.7 copy-start.11
  188.5 4.7 copy-start.20
  194.4 95.5 %copy-start.9 = (bf16[128,512]{1,0:T(8,128)(2,1)S(1)}, bf16[128,512]{1,0:T(8,128)(2,1)}, u32[]{:S(2)}) copy-start(bf16[128,512]{1,0:T(8,128)(2,1)} %param.18) | copy-start | bytes 393220
  194.5 102.4 %copy-start.19 = (pred[128]{0:T(512)(128)(4,1)S(1)}, pred[128]{0:T(512)(128)(4,1)}, u32[]{:S(2)}) copy-start(pred[128]{0:T(512)(128)(4,1)} %copy-done.18) | copy-start | bytes 388
  194.5 322.8 %all-reduce.7.cloned.1.call-start = ((), (), s32[]{:S(2)}) async-start(), calls=%async_computation.10 | async-start | bytes 11010048 | tf_op jit(solution)/shard_map/psum | solution.py:14
  290.0 31.4 %copy-start.5 = (bf16[128,512]{1,0:T(8,128)(2,1)S(1)}, bf16[128,512]{1,0:T(8,128)(2,1)}, u32[]{:S(2)}) copy-start(bf16[128,512]{1,0:T(8,128)(2,1)} %get-tuple-element.310) | copy-start | bytes 393220
  292.1 21.0 %all-to-all-start.4 = ((f32[32,10,128]{2,1,0:T(8,128)}), f32[32,10,128]{2,1,0:T(8,128)}, u32[]{:S(2)}, u32[]{:S(2)}) async-start(f32[32,10,128]{2,1,0:T(8,128)} %reshape.392), calls=%async_computation.4 | async-start | bytes 524288 | tf_op jit(solution)/shard_map/all_to_all | solution.py:292
  313.1 59.7 %all-to-all-start.3 = ((f32[32,10,512]{2,1,0:T(8,128)}), f32[32,10,512]{2,1,0:T(8,128)S(1)}, u32[]{:S(2)}, u32[]{:S(2)}) async-start(f32[32,10,512]{2,1,0:T(8,128)} %reshape.390), calls=%async_computation.3 | async-start | bytes 2097152 | tf_op jit(solution)/shard_map/all_to_all | solution.py:291
  517.3 4.9 copy-start.6
  517.3 6.0 %copy-start.12 = (f32[128,512]{1,0:T(8,128)S(1)}, f32[128,512]{1,0:T(8,128)}, u32[]{:S(2)}) copy-start(f32[128,512]{1,0:T(8,128)} %get-tuple-element.306) | copy-start | bytes 786436
Sparse Core Ops, SparseCore 0:
  63.3 21.6 all-gather.4
  87.4 23.3 all-gather.6
  112.7 23.3 all-gather.10
  137.9 23.3 all-gather.8
  194.6 95.3 all-reduce.4
  292.4 224.8 all-reduce.6
